TPU v7x, 128 devices: a whole 4x4x4 slice. The times are simulated.
128 devices in a mesh: cache: 32 (over x, y, z_lo), batch: 4 (over z_hi, core).
Axes of the slice: x: 4, y: 4, z: 4 (z_hi: 2, z_lo: 2; z = z_hi * 2 + z_lo), core: 2. Of those that a mesh axis runs over, the one named last changes fastest.
Arguments:
- queries: bfloat16 [3, 4096, 768], P(None, 'batch')
- positives: int32 [3, 4096], P(None, 'batch'), may hold values from 0 to 511
- block_list: int32 [3, 32, 192], P(None, 'batch'), may hold values from 0 to 255
- block_count: int32 [3, 32], P(None, 'batch'), may hold values from 1 to 192
- refresh_owner: int32 [3], replicated, may hold values from 0 to 31, as said below
- cache: float32 [32768, 768], P('cache'), may hold values from -6 to 6
- fresh: float32 [16384, 768], P('cache')
Outputs:
- query_grad: float32 [3, 4096, 768], P(None, ('batch', 'cache'))
- cache_grad: float32 [32768, 768], P('cache')
Inputs may be any that keep to these rules, and one draw needn't show every extreme that they name: `refresh_owner`: 3 different owners; owner 0 and owner 32 - 1 are always among them.
All inputs are finite; a program needn't handle non-finite values.
Results may differ from a plain program's by a relative error of at most 0.0003.
Values sent between devices are 32-bit elements; how exact they have to be, the bound alone decides.
A program may use at most 128 MiB of HBM per device.

v0:
```python
import math
import jax
import jax.numpy as jnp
from jax import lax
from jax.sharding import PartitionSpec as P

BLK = 128


def broadcast(block, axis, holder):
    block = jnp.where(lax.axis_index(axis) == holder, block, jnp.zeros_like(block))
    return lax.psum(block, axis)


def on_device(queries, positives, block_list, block_count, refresh_owner, cache, fresh):
    highest = lax.Precision.HIGHEST
    steps, group_rows, width = queries.shape
    cache_rows = cache.shape[0]
    slab_rows = fresh.shape[0]
    owners = lax.axis_size("cache")
    own_index = lax.axis_index("cache")
    share = group_rows // owners
    home_start = own_index * share
    group_blocks = block_list.shape[1]
    list_width = block_list.shape[2]
    own_blocks = cache_rows // BLK
    scale = 2.0 / math.sqrt(width)
    block_ids = own_index * own_blocks + jnp.arange(own_blocks, dtype=jnp.int32)
    current = cache
    grad_total = jnp.zeros((cache_rows, width), jnp.float32)
    results = []
    for step in range(steps):
        owner = refresh_owner[step]
        is_owner = owner == own_index
        refreshed = jnp.concatenate([fresh, current[slab_rows:]], axis=0)
        current = jnp.where(is_owner, refreshed, current)
        valid = jnp.arange(list_width, dtype=jnp.int32)[None, :] < block_count[step][:, None]
        hits = (block_list[step][:, :, None] == block_ids[None, None, :]) & valid[:, :, None]
        member = jnp.any(hits, axis=1)
        mask = jnp.broadcast_to(member[:, None, :, None], (group_blocks, BLK, own_blocks, BLK))
        mask = mask.reshape(group_rows, cache_rows)
        query_rows = queries[step].astype(jnp.float32)
        scores = scale * jnp.dot(query_rows, current.T, precision=highest)
        scores = jnp.where(mask, scores, -1e30)
        peak = jnp.max(scores, axis=1)
        slab = broadcast(fresh, "cache", owner)
        home_queries = lax.dynamic_slice_in_dim(query_rows, home_start, share, 0)
        slab_scores = scale * jnp.dot(home_queries, slab.T, precision=highest)
        filler = jnp.full((group_rows,), -1e30, jnp.float32)
        slab_peak = lax.dynamic_update_slice_in_dim(
            filler, jnp.max(slab_scores, axis=1), home_start, 0
        )
        peak = jnp.maximum(peak, slab_peak)
        top = lax.pmax(peak, "cache")
        total = jnp.sum(jnp.where(mask, jnp.exp(scores - top[:, None]), 0.0), axis=1)
        home_top = lax.dynamic_slice_in_dim(top, home_start, share, 0)
        slab_total = jnp.sum(jnp.exp(slab_scores - home_top[:, None]), axis=1)
        home_part = lax.dynamic_slice_in_dim(total, home_start, share, 0) + slab_total
        total = lax.dynamic_update_slice_in_dim(total, home_part, home_start, 0)
        total = lax.psum(total, "cache")
        lse = top + jnp.log(total)
        probs = jnp.exp(scores - lse[:, None])
        home_lse = lax.dynamic_slice_in_dim(lse, home_start, share, 0)
        slab_probs = jnp.exp(slab_scores - home_lse[:, None])
        home_pos = lax.dynamic_slice_in_dim(positives[step], home_start, share, 0)
        home_term = jnp.dot(slab_probs, slab, precision=highest) - jnp.take(slab, home_pos, axis=0)
        term = jnp.dot(probs, current, precision=highest)
        mine = lax.psum_scatter(term, "cache", scatter_dimension=0, tiled=True)
        mine = mine + home_term
        results.append(mine)
        step_grad = lax.dot_general(probs, query_rows, (((0,), (0,)), ((), ())), precision=highest)
        grad_total = grad_total + lax.psum(step_grad, "batch")
    return (jnp.stack(results, axis=0), grad_total)


def solution(mesh):
    return jax.shard_map(
        on_device,
        mesh=mesh,
        in_specs=(
            P(None, "batch", None),
            P(None, "batch"),
            P(None, "batch", None),
            P(None, "batch"),
            P(),
            P("cache", None),
            P("cache", None),
        ),
        out_specs=(P(None, ("batch", "cache"), None), P("cache", None)),
        check_vma=False,
    )
```

profile of v0, /device:TPU:1, one launch (start us, length us, event | category | flops | bytes accessed | tf_op | source)
XLA Modules:
  0.0 1261.3 jit_solution(4495534913368518108)
XLA Ops:
  7.2 1.4 fusion.62
  10.5 3.7 broadcast_select_fusion.2
  16.5 1.9 copy-done.11
  18.4 0.4 fusion.6
  18.9 0.4 fusion.7
  19.3 1.1 copy-done.1
  20.5 1.7 copy-done.4
  22.3 0.5 copy-done.24
  23.0 0.6 and_reduce_fusion.2
  23.8 4.8 fusion.60
  28.6 0.3 broadcast_in_dim.29
  29.0 9.3 fusion.65
  38.6 7.3 fusion.67
  46.3 1.0 copy-done.21
  47.2 7.4 fusion.63
  54.7 270.4 %all-reduce.8.cloned.1.call-done = (f32[512,768]{1,0:T(8,128)}, f32[512,768]{1,0:T(8,128)}, f32[512,768]{1,0:T(8,128)}) async-done(((f32[512,768]{1,0:T(8,128)}, f32[512,768]{1,0:T(8,128)}, f32[512,768]{1,0:T(8,128)}), (f32[512,768]{1,0:T(8,128)}, f32[512,768]{1,0:T(8,128)}, f32[512,768]{1,0:T(8,128)})) %all-reduce.8.cloned.1.call-update) | async-done | bytes 4718608 | tf_op jit(solution)/shard_map/psum | solution.py:12
  325.1 2.5 fusion.64
  327.9 2.4 fusion.66
  330.5 1.8 fusion.68
  332.4 0.6 dynamic_update_slice.18
  333.0 130.1 %all-reduce.2 = (f32[1024]{0:T(1024)S(1)}, f32[1024]{0:T(1024)S(1)}, f32[1024]{0:T(1024)S(1)}) all-reduce(f32[1024]{0:T(1024)S(1)} %max.17, f32[1024]{0:T(1024)S(1)} %max.16, f32[1024]{0:T(1024)S(1)} %max.15), channel_id=1, replica_groups=mesh['cache'=32,'batch'=4] {'cache'}, use_global_device_ids=true, to_apply=%region_22.24 | all-reduce | flops 3072 | bytes 24576 | tf_op jit(solution)/shard_map/pmax | solution.py:54
  463.2 3.7 select_reduce_fusion
  466.9 1.1 select_reduce_fusion.1
  468.2 0.9 copy-done.16
  469.3 1.1 select_reduce_fusion.2
  471.5 124.2 %all-reduce = (f32[1024]{0:T(1024)S(1)}, f32[1024]{0:T(1024)S(1)}, f32[1024]{0:T(1024)S(1)}) all-reduce(f32[1024]{0:T(1024)S(1)} %add_dynamic-update-slice_fusion, f32[1024]{0:T(1024)S(1)} %add_dynamic-update-slice_fusion.1, f32[1024]{0:T(1024)S(1)} %add_dynamic-update-slice_fusion.2), channel_id=1, replica_groups=mesh['cache'=32,'batch'=4] {'cache'}, use_global_device_ids=true, to_apply=%region_25.27 | all-reduce | flops 3072 | bytes 24576 | tf_op jit(solution)/shard_map/psum | solution.py:60
  595.8 14.5 %fusion.5 = f32[1024,768]{1,0:T(8,128)} fusion(f32[1024,1024]{0,1:T(8,128)} %get-tuple-element.40, f32[1024]{0:T(1024)S(1)} %log_add_fusion, f32[1024,768]{1,0:T(8,128)} %copy-done.4, f32[512,768]{1,0:T(8,128)S(1)} %copy-done, f32[512,768]{1,0:T(8,128)S(1)} %copy-done.13, pred[]{:T(512)S(6)} %eq.73), kind=kOutput, calls=%fused_computation.20 | convolution fusion | flops 9666297856 | bytes 13635585 | tf_op jit(solution)/shard_map/dot_general | solution.py:67
  610.4 1.8 copy-done.6
  612.2 13.5 %fusion.3 = f32[1024,768]{1,0:T(8,128)} fusion(f32[1024,768]{1,0:T(8,128)S(1)} %copy-done.6, f32[1024,1024]{0,1:T(8,128)} %get-tuple-element.44, f32[1024]{0:T(1024)S(1)} %log_add_fusion.1), kind=kOutput, calls=%fused_computation.18 | convolution fusion | flops 9664724992 | bytes 10489856 | tf_op jit(solution)/shard_map/dot_general | solution.py:67
  625.8 1.8 copy-done.3
  627.6 13.4 %fusion.1 = f32[1024,768]{1,0:T(8,128)} fusion(f32[1024,768]{1,0:T(8,128)S(1)} %copy-done.3, f32[1024,1024]{0,1:T(8,128)} %get-tuple-element.48, f32[1024]{0:T(1024)S(1)} %log_add_fusion.2), kind=kOutput, calls=%fused_computation.16 | convolution fusion | flops 9664724992 | bytes 10489856 | tf_op jit(solution)/shard_map/dot_general | solution.py:67
  641.1 8.2 fusion
  649.3 7.2 fusion.2
  656.6 8.8 add_add_fusion
  665.7 0.6 dynamic_slice.75
  666.3 0.6 dynamic_slice.68
  667.1 2.7 gather_fusion.2
  669.8 1.2 gather_fusion.1
  671.0 0.6 gather_fusion
  671.6 151.8 %reduce-scatter.8.cloned.1.call-done = f32[32,768]{1,0:T(8,128)} async-done(((f32[1024,768]{1,0:T(8,128)}), f32[32,768]{1,0:T(8,128)}) %reduce-scatter.8.cloned.1.call-update) | async-done | bytes 98320 | tf_op jit(solution)/shard_map/reduce_scatter | solution.py:68
  823.4 2.7 fusion.24
  826.1 162.2 %reduce-scatter.6.cloned.1.call-done = f32[32,768]{1,0:T(8,128)} async-done(((f32[1024,768]{1,0:T(8,128)}), f32[32,768]{1,0:T(8,128)}) %reduce-scatter.6.cloned.1.call-update) | async-done | bytes 98320 | tf_op jit(solution)/shard_map/reduce_scatter | solution.py:68
  988.3 2.6 fusion.26
  990.9 161.3 %reduce-scatter.4.cloned.1.call-done = f32[32,768]{1,0:T(8,128)} async-done(((f32[1024,768]{1,0:T(8,128)}), f32[32,768]{1,0:T(8,128)}) %reduce-scatter.4.cloned.1.call-update) | async-done | bytes 98320 | tf_op jit(solution)/shard_map/reduce_scatter | solution.py:68
  1152.2 1.9 fusion.28
  1154.1 1.6 pad_maximum_fusion.3
  1155.7 95.0 %all-reduce.6.cloned.1.call-done = f32[1024,768]{1,0:T(8,128)} async-done(((f32[1024,768]{1,0:T(8,128)}), f32[1024,768]{1,0:T(8,128)}) %all-reduce.6.cloned.1.call-update) | async-done | bytes 3145744 | tf_op jit(solution)/shard_map/psum | solution.py:72
  1250.7 3.8 copy.31
  (99 shorter events, 4.2 us)
Async XLA Ops:
  7.2 317.9 %all-reduce.8.cloned.1.call-start = ((), (), s32[]{:S(2)}) async-start(), calls=%async_computation.7 | async-start | bytes 9437184 | tf_op jit(solution)/shard_map/psum | solution.py:12
  14.2 2.3 copy-start
  14.2 2.3 slice-start
  14.3 809.2 %reduce-scatter.8.cloned.1.call-start = ((), (), s32[]{:S(2)}) async-start(), calls=%async_computation.5 | async-start | bytes 3244032 | tf_op jit(solution)/shard_map/reduce_scatter | solution.py:68
  16.5 1.9 copy-start.11
  18.8 1.7 copy-start.1
  20.5 1.7 copy-start.4
  22.1 0.7 copy-start.24
  22.1 0.8 copy-start.22
  22.2 24.0 %copy-start.12 = (f32[512,768]{1,0:T(8,128)}, f32[512,768]{1,0:T(8,128)S(1)}, u32[]{:S(2)}) copy-start(f32[512,768]{1,0:T(8,128)S(1)} %slice.79) | copy-start | bytes 4718596
  23.8 5.1 copy-start.5
  28.6 10.0 slice-start.1
  28.9 9.3 copy-start.17
  28.9 9.7 copy-start.2
  28.9 9.7 slice-start.2
  38.6 7.3 copy-start.19
  46.3 1.0 copy-start.21
  325.1 5.5 copy-start.8
  332.3 134.6 %copy-start.18 = (pred[8,128,8,128]{1,0,3,2:T(8,128)(4,1)S(1)}, pred[8,128,8,128]{1,0,3,2:T(8,128)(4,1)}, u32[]{:S(2)}) copy-start(pred[8,128,8,128]{1,0,3,2:T(8,128)(4,1)} %copy-done.17) | copy-start | bytes 3145732
  463.1 3.9 copy-start.14
  466.8 2.2 copy-start.16
  466.8 2.5 copy-start.20
  468.1 127.7 %copy-start.13 = (f32[512,768]{1,0:T(8,128)S(1)}, f32[512,768]{1,0:T(8,128)}, u32[]{:S(2)}) copy-start(f32[512,768]{1,0:T(8,128)} %copy-done.12) | copy-start | bytes 4718596
  610.3 1.9 copy-start.6
  610.3 378.0 %reduce-scatter.6.cloned.1.call-start = ((), (), s32[]{:S(2)}) async-start(), calls=%async_computation.4 | async-start | bytes 3244032 | tf_op jit(solution)/shard_map/reduce_scatter | solution.py:68
  625.7 1.9 copy-start.3
  625.8 526.4 %reduce-scatter.4.cloned.1.call-start = ((), (), s32[]{:S(2)}) async-start(), calls=%async_computation.3 | async-start | bytes 3244032 | tf_op jit(solution)/shard_map/reduce_scatter | solution.py:68
  641.0 609.7 %all-reduce.6.cloned.1.call-start = ((), (), s32[]{:S(2)}) async-start(), calls=%async_computation.6 | async-start | bytes 6291456 | tf_op jit(solution)/shard_map/psum | solution.py:72
  641.1 8.2 copy-start.15
  649.3 7.3 copy-start.7
  656.6 8.8 copy-start.23
  665.4 4.4 copy-start.10
  665.4 5.6 copy-start.9
Sparse Core Ops, SparseCore 0:
  14.4 310.6 all-reduce.7
  610.4 212.9 reduce-scatter.7
  826.5 161.7 reduce-scatter.5
  990.6 161.5 reduce-scatter.3
  1154.7 95.9 all-reduce.5
where the time goes:
time: 1260 us
  waiting for transfers between devices  841 us (67%)
  blocking collectives  254 us (20%)
  matrix products  104 us (8%)
  local copies, waits for them, and re-layouts  29.7 us (2%)
  between operations  18.6 us (1%)
  other arithmetic  14.1 us (1%)
    reduce_scatter x3, waiting for transfers between devices, on_device(): mine = lax.psum_scatter(term, 'cache', scatter_dimension=0, tiled=True)  475 us
    psum x1, waiting for transfers between devices, broadcast(): return lax.psum(block, axis)  270 us
    pmax x1, blocking collectives, on_device(): top = lax.pmax(peak, 'cache')  130 us
    psum x1, blocking collectives, on_device(): total = lax.psum(total, 'cache')  124 us
    psum x1, waiting for transfers between devices, on_device(): grad_total = grad_total + lax.psum(step_grad, 'batch')  95 us
    dot_general x3, matrix products, on_device(): term = jnp.dot(probs, current, precision=highest)  41.5 us
  transfers between devices with their start and end apart: 5, of which 5 were waited for; matrix products, arithmetic and copies ran while one was open for 8% of the time, Pallas kernels for 0%

commit v1 on v0

--- a/solution.py
+++ b/solution.py
@@ -69,7 +69,7 @@
         mine = mine + home_term
         results.append(mine)
         step_grad = lax.dot_general(probs, query_rows, (((0,), (0,)), ((), ())), precision=highest)
-        grad_total = grad_total + lax.psum(step_grad, "batch")
+        grad_total = grad_total + jnp.sum(lax.all_gather(step_grad, "batch"), axis=0)
     return (jnp.stack(results, axis=0), grad_total)
 
 

time: 1260 us -> 1460 us (1.16)
  waiting for transfers between devices: 841 us -> 1010 us
  other arithmetic: 14.1 us -> 41.9 us
    all_gather x0 -> x3, waiting for transfers between devices: none -> 266 us  [on_device(): lax.all_gather(step_grad, 'batch')]
    psum x1 -> x0, waiting for transfers between devices: 95 us -> none  [on_device(): grad_total = grad_total + lax.psum(step_grad, 'batch')]
    reduce_sum x0 -> x3, other arithmetic: none -> 20.7 us  [on_device(): jnp.sum(lax.all_gather(step_grad, 'batch'), axis=0)]
  transfers between devices with their start and end apart: 5 -> 7, of which waited for: 5 -> 7; matrix products, arithmetic and copies ran while one was open for 8% -> 8% of each run, Pallas kernels for 0% -> 0%
where the time goes in v1:
time: 1460 us; the launch traced here: 1450 us
  waiting for transfers between devices  1010 us (69%)
  blocking collectives  253 us (17%)
  matrix products  110 us (8%)
  other arithmetic  41.9 us (3%)
  local copies, waits for them, and re-layouts  22 us (2%)
  between operations  18.9 us (1%)
    reduce_scatter x3, waiting for transfers between devices, on_device(): mine = lax.psum_scatter(term, 'cache', scatter_dimension=0, tiled=True)  474 us
    psum x1, waiting for transfers between devices, broadcast(): return lax.psum(block, axis)  269 us
    all_gather x3, waiting for transfers between devices, on_device(): lax.all_gather(step_grad, 'batch')  266 us
    pmax x1, blocking collectives, on_device(): top = lax.pmax(peak, 'cache')  128 us
    psum x1, blocking collectives, on_device(): total = lax.psum(total, 'cache')  125 us
    dot_general x3, matrix products, on_device(): term = jnp.dot(probs, current, precision=highest)  42.7 us
  transfers between devices with their start and end apart: 7, of which 7 were waited for; matrix products, arithmetic and copies ran while one was open for 8% of the time, Pallas kernels for 0%

profile of v1, /device:TPU:1, one launch (start us, length us, event | category | flops | bytes accessed | tf_op | source)
XLA Modules:
  0.0 1454.9 jit_solution(7316383097562187674)
XLA Ops:
  7.2 1.4 fusion.60
  10.6 3.7 broadcast_select_fusion.2
  16.7 1.9 copy-done.7
  19.1 2.4 fusion.7
  21.6 1.5 slice.79
  23.3 0.6 and_reduce_fusion.2
  24.1 4.6 fusion.58
  29.1 9.7 fusion.63
  39.2 7.3 fusion.65
  46.9 1.0 copy-done.16
  47.9 9.2 fusion.61
  57.1 269.1 %all-reduce.5.cloned.1.call-done = (f32[512,768]{1,0:T(8,128)}, f32[512,768]{1,0:T(8,128)}, f32[512,768]{1,0:T(8,128)}) async-done(((f32[512,768]{1,0:T(8,128)}, f32[512,768]{1,0:T(8,128)}, f32[512,768]{1,0:T(8,128)}), (f32[512,768]{1,0:T(8,128)}, f32[512,768]{1,0:T(8,128)}, f32[512,768]{1,0:T(8,128)})) %all-reduce.5.cloned.1.call-update) | async-done | bytes 4718608 | tf_op jit(solution)/shard_map/psum | solution.py:12
  326.1 2.5 fusion.62
  328.9 2.4 fusion.64
  331.6 1.8 fusion.66
  333.4 0.5 dynamic_update_slice.18
  333.9 128.4 %all-reduce.2 = (f32[1024]{0:T(1024)S(1)}, f32[1024]{0:T(1024)S(1)}, f32[1024]{0:T(1024)S(1)}) all-reduce(f32[1024]{0:T(1024)S(1)} %max.17, f32[1024]{0:T(1024)S(1)} %max.16, f32[1024]{0:T(1024)S(1)} %max.15), channel_id=1, replica_groups=mesh['cache'=32,'batch'=4] {'cache'}, use_global_device_ids=true, to_apply=%region_22.24 | all-reduce | flops 3072 | bytes 24576 | tf_op jit(solution)/shard_map/pmax | solution.py:54
  462.3 3.7 select_reduce_fusion
  466.1 1.1 select_reduce_fusion.1
  467.3 0.9 copy-done.11
  468.5 1.1 select_reduce_fusion.2
  470.7 124.6 %all-reduce = (f32[1024]{0:T(1024)S(1)}, f32[1024]{0:T(1024)S(1)}, f32[1024]{0:T(1024)S(1)}) all-reduce(f32[1024]{0:T(1024)S(1)} %add_dynamic-update-slice_fusion, f32[1024]{0:T(1024)S(1)} %add_dynamic-update-slice_fusion.1, f32[1024]{0:T(1024)S(1)} %add_dynamic-update-slice_fusion.2), channel_id=1, replica_groups=mesh['cache'=32,'batch'=4] {'cache'}, use_global_device_ids=true, to_apply=%region_25.27 | all-reduce | flops 3072 | bytes 24576 | tf_op jit(solution)/shard_map/psum | solution.py:60
  595.3 14.5 fusion.5
  609.9 14.8 %fusion.3 = f32[1024,768]{1,0:T(8,128)} fusion(f32[1024,768]{1,0:T(8,128)} %fusion.7, f32[1024,1024]{0,1:T(8,128)} %get-tuple-element.44, f32[1024]{0:T(1024)S(1)} %log_add_fusion.1), kind=kOutput, calls=%fused_computation.18 | convolution fusion | flops 9664724992 | bytes 10489856 | tf_op jit(solution)/shard_map/dot_general | solution.py:67
  624.8 1.8 copy-done.3
  626.6 13.4 fusion.1
  640.1 9.2 fusion.4
  649.3 9.0 fusion
  658.4 9.0 fusion.2
  667.8 0.6 dynamic_slice.75
  668.4 0.6 dynamic_slice.68
  669.0 2.7 gather_fusion.2
  671.7 1.2 gather_fusion.1
  673.0 0.6 gather_fusion
  673.6 148.3 %reduce-scatter.8.cloned.1.call-done = f32[32,768]{1,0:T(8,128)} async-done(((f32[1024,768]{1,0:T(8,128)}), f32[32,768]{1,0:T(8,128)}) %reduce-scatter.8.cloned.1.call-update) | async-done | bytes 98320 | tf_op jit(solution)/shard_map/reduce_scatter | solution.py:68
  821.9 2.4 fusion.22
  824.3 163.4 %reduce-scatter.6.cloned.1.call-done = f32[32,768]{1,0:T(8,128)} async-done(((f32[1024,768]{1,0:T(8,128)}), f32[32,768]{1,0:T(8,128)}) %reduce-scatter.6.cloned.1.call-update) | async-done | bytes 98320 | tf_op jit(solution)/shard_map/reduce_scatter | solution.py:68
  987.8 2.6 fusion.24
  990.4 162.3 %reduce-scatter.4.cloned.1.call-done = f32[32,768]{1,0:T(8,128)} async-done(((f32[1024,768]{1,0:T(8,128)}), f32[32,768]{1,0:T(8,128)}) %reduce-scatter.4.cloned.1.call-update) | async-done | bytes 98320 | tf_op jit(solution)/shard_map/reduce_scatter | solution.py:68
  1152.7 1.9 fusion.26
  1154.6 1.6 pad_maximum_fusion.3
  1156.2 104.6 %all-gather.11.cloned.1.call-done = f32[4096,768]{1,0:T(8,128)} async-done(((f32[1024,768]{1,0:T(8,128)}), f32[4096,768]{1,0:T(8,128)}) %all-gather.11.cloned.1.call-update) | async-done | bytes 12582928 | tf_op jit(solution)/shard_map/all_gather | solution.py:72
  1260.8 5.8 reduce_sum.89
  1266.6 81.4 %all-gather.7.cloned.1.call-done = f32[4096,768]{1,0:T(8,128)} async-done(((f32[1024,768]{1,0:T(8,128)}), f32[4096,768]{1,0:T(8,128)}) %all-gather.7.cloned.1.call-update) | async-done | bytes 12582928 | tf_op jit(solution)/shard_map/all_gather | solution.py:72
  1348.0 7.5 reduce_sum.87
  1355.5 79.8 %all-gather.9.cloned.1.call-done = f32[4096,768]{1,0:T(8,128)} async-done(((f32[1024,768]{1,0:T(8,128)}), f32[4096,768]{1,0:T(8,128)}) %all-gather.9.cloned.1.call-update) | async-done | bytes 12582928 | tf_op jit(solution)/shard_map/all_gather | solution.py:72
  1435.3 7.5 reduce_sum.88
  1442.8 5.1 add_add_fusion
  (98 shorter events, 5.1 us)
Async XLA Ops:
  7.2 319.0 %all-reduce.5.cloned.1.call-start = ((), (), s32[]{:S(2)}) async-start(), calls=%async_computation.9 | async-start | bytes 9437184 | tf_op jit(solution)/shard_map/psum | solution.py:12
  14.3 2.3 copy-start
  14.3 2.3 slice-start
  14.4 807.5 %reduce-scatter.8.cloned.1.call-start = ((), (), s32[]{:S(2)}) async-start(), calls=%async_computation.5 | async-start | bytes 3244032 | tf_op jit(solution)/shard_map/reduce_scatter | solution.py:68
  16.6 1.9 copy-start.7
  18.9 2.6 copy-start.1
  21.6 1.6 copy-start.19
  21.6 1.7 copy-start.17
  23.1 23.8 %copy-start.8 = (f32[512,768]{1,0:T(8,128)}, f32[512,768]{1,0:T(8,128)S(1)}, u32[]{:S(2)}) copy-start(f32[512,768]{1,0:T(8,128)S(1)} %slice.79) | copy-start | bytes 4718596
  28.7 10.4 slice-start.1
  29.1 9.7 copy-start.12
  29.1 10.1 copy-start.2
  29.1 10.1 slice-start.2
  39.2 7.3 copy-start.14
  46.8 1.0 copy-start.16
  326.1 5.5 copy-start.4
  333.4 132.7 %copy-start.13 = (pred[8,128,8,128]{1,0,3,2:T(8,128)(4,1)S(1)}, pred[8,128,8,128]{1,0,3,2:T(8,128)(4,1)}, u32[]{:S(2)}) copy-start(pred[8,128,8,128]{1,0,3,2:T(8,128)(4,1)} %copy-done.12) | copy-start | bytes 3145732
  462.3 3.9 copy-start.10
  466.0 2.2 copy-start.11
  466.0 2.5 copy-start.15
  467.3 128.1 %copy-start.9 = (f32[512,768]{1,0:T(8,128)S(1)}, f32[512,768]{1,0:T(8,128)}, u32[]{:S(2)}) copy-start(f32[512,768]{1,0:T(8,128)} %copy-done.8) | copy-start | bytes 4718596
  609.9 377.9 %reduce-scatter.6.cloned.1.call-start = ((), (), s32[]{:S(2)}) async-start(), calls=%async_computation.4 | async-start | bytes 3244032 | tf_op jit(solution)/shard_map/reduce_scatter | solution.py:68
  624.7 1.9 copy-start.3
  624.7 527.9 %reduce-scatter.4.cloned.1.call-start = ((), (), s32[]{:S(2)}) async-start(), calls=%async_computation.3 | async-start | bytes 3244032 | tf_op jit(solution)/shard_map/reduce_scatter | solution.py:68
  640.0 620.8 %all-gather.11.cloned.1.call-start = ((), (), s32[]{:S(2)}) async-start(), calls=%async_computation.8 | async-start | bytes 15728640 | tf_op jit(solution)/shard_map/all_gather | solution.py:72
  649.3 698.7 %all-gather.7.cloned.1.call-start = ((), (), s32[]{:S(2)}) async-start(), calls=%async_computation.6 | async-start | bytes 15728640 | tf_op jit(solution)/shard_map/all_gather | solution.py:72
  658.4 776.9 %all-gather.9.cloned.1.call-start = ((), (), s32[]{:S(2)}) async-start(), calls=%async_computation.7 | async-start | bytes 15728640 | tf_op jit(solution)/shard_map/all_gather | solution.py:72
  658.4 9.1 copy-start.18
  667.5 4.3 copy-start.6
  667.5 5.5 copy-start.5
Sparse Core Ops, SparseCore 0:
  14.5 311.6 all-reduce.4
  610.0 211.8 reduce-scatter.7
  824.4 163.3 reduce-scatter.5
  990.6 162.0 reduce-scatter.3
  1154.3 106.5 all-gather.10
  1262.5 85.4 all-gather.6
  1349.8 85.4 all-gather.8
